TPU v7x, 256 devices: a whole 4x4x8 slice. The times are simulated.
256 devices in a mesh: wide: 16 (over x_lo, y, core), narrow: 16 (over z, x_hi).
Axes of the slice: x: 4 (x_hi: 2, x_lo: 2; x = x_hi * 2 + x_lo), y: 4, z: 8, core: 2. Of those that a mesh axis runs over, the one named last changes fastest.
Arguments:
- coarse_basis: bfloat16 [32, 96, 3, 64, 8, 128], P('wide', None, None, 'narrow')
- material_ids: int32 [32, 64, 8, 128], P('wide', 'narrow'), may hold values from 0 to 15
- lame_table: bfloat16 [2, 16], replicated, may hold values from 0.5 to 4
- coarse_ids: int32 [32, 96], P('wide'), may hold values from 0 to 127, as said below
- coarse_slab: bfloat16 [98304, 2048], P('wide', 'narrow'), may hold values from -0.5 to 2.5, as said below
- panel_owner: int32 [1], replicated, may hold values from 0 to 14
Outputs:
- factored: bfloat16 [98304, 2048], P('wide', 'narrow')
- galerkin: float32 [32, 96, 96], P('wide')
Inputs may be any that keep to these rules, and one draw needn't show every extreme that they name: `coarse_ids`: the 96 numbers of a row are distinct. `coarse_slab`: for every column block t, the 128 x 128 block whose rows begin at t * 6144 is symmetric positive definite.
All inputs are finite; a program needn't handle non-finite values.
Results may differ from a plain program's by a relative error of at most 0.001.
The roundings to bfloat16 on the way count: a program that leaves them out, or rounds other values in their place, can miss the bound.
Values may be sent and summed in bfloat16 or wider, within the bound.
A program may use at most 192 MiB of HBM per device.

v0:
```python
import jax
import jax.numpy as jnp
from jax import lax
from jax.sharding import PartitionSpec as P


def padded_2(x, sides, width):
    for axis, dim in sides:
        count, length = (lax.axis_size(axis), x.shape[dim])
        up = [(i, (i + 1) % count) for i in range(count - 1)]
        down = [(j, i) for i, j in up]
        last = lax.slice_in_dim(x, length - width, length, axis=dim)
        initial = lax.slice_in_dim(x, 0, width, axis=dim)
        before = lax.ppermute(last, axis, up)
        after = lax.ppermute(initial, axis, down)
        x = jnp.concatenate([before, x, after], axis=dim)
    return x


def broadcast(value, axis, source):
    kept = jnp.where(lax.axis_index(axis) == source, value, 0).astype(value.dtype)
    return lax.psum(kept, axis)


def lower_inverse(lower):
    identity = jnp.eye(lower.shape[0], dtype=lower.dtype)
    return lax.linalg.triangular_solve(lower, identity, left_side=True, lower=True)


def lame_fields(material_ids, lame_table):
    values = lame_table.astype(jnp.float32)
    shear = jnp.zeros(material_ids.shape, jnp.float32)
    dilatation = jnp.zeros(material_ids.shape, jnp.float32)
    for material in range(values.shape[1]):
        chosen = material_ids == material
        shear = jnp.where(chosen, values[0, material], shear)
        dilatation = jnp.where(chosen, values[1, material], dilatation)
    return (shear, dilatation)


def shifted(field, axis, step):
    length = field.shape[axis]
    border = jnp.zeros_like(lax.slice_in_dim(field, 0, 1, axis=axis))
    if step > 0:
        return jnp.concatenate([lax.slice_in_dim(field, 1, length, axis=axis), border], axis=axis)
    return jnp.concatenate([border, lax.slice_in_dim(field, 0, length - 1, axis=axis)], axis=axis)


def face_weight(coeff_one, coeff_two, direction):
    shear = 0.5 * (coeff_one[:, 0:1] + coeff_two[:, 0:1])
    dilate = 0.5 * (coeff_one[:, 1:2] + coeff_two[:, 1:2])
    unit = (jnp.arange(3) == direction).astype(shear.dtype).reshape(1, 1, 3, 1, 1, 1)
    return shear + unit * (dilate + shear)


def operator_image(padded, coeff):
    centre = padded[:, :, :, 1:-1]
    coeff_centre = coeff[:, :, :, 1:-1]
    pairs = [
        (padded[:, :, :, 2:], coeff[:, :, :, 2:], 0),
        (padded[:, :, :, :-2], coeff[:, :, :, :-2], 0),
    ]
    for axis, direction in ((4, 1), (5, 2)):
        for step in (1, -1):
            pairs.append(
                (shifted(centre, axis, step), shifted(coeff_centre, axis, step), direction)
            )
    image = jnp.zeros(centre.shape, centre.dtype)
    for other, other_coeff, direction in pairs:
        image = image + face_weight(coeff_centre, other_coeff, direction) * (centre - other)
    return image


def galerkin_of(left_field, right_field):
    subs, funcs = (left_field.shape[0], left_field.shape[1])
    return jnp.einsum(
        "sak,sbk->sab",
        left_field.reshape(subs, funcs, -1),
        right_field.reshape(subs, funcs, -1),
        precision=lax.Precision.HIGHEST,
    )


def diagonal_factor(diagonal):
    diagonal = 0.5 * (diagonal + diagonal.T)
    lower = jnp.linalg.cholesky(diagonal)
    return (lower, lower_inverse(lower))


def panel_factor(column, lower, inverse, wide_index, owner, stride):
    solved = jnp.dot(column.astype(jnp.float32), inverse.T, precision=lax.Precision.HIGHEST)
    rows = lax.broadcasted_iota(jnp.int32, solved.shape, 0)
    head = rows < lower.shape[0]
    own_block = jnp.pad(lower, ((0, solved.shape[0] - lower.shape[0]), (0, 0)))
    diagonal_rows = head & (wide_index == owner * stride)
    earlier = head & (wide_index % stride == 0) & (wide_index // stride < owner)
    solved = jnp.where(diagonal_rows, own_block, solved)
    solved = jnp.where(earlier, 0.0, solved)
    return solved.astype(jnp.bfloat16)


def on_device(coarse_basis, material_ids, lame_table, coarse_ids, coarse_slab, panel_owner):
    narrow_count = lax.axis_size("narrow")
    stride = lax.axis_size("wide") // narrow_count
    wide_index = lax.axis_index("wide")
    narrow_index = lax.axis_index("narrow")
    owner = panel_owner[0]
    block = coarse_slab.shape[1]
    shear, dilatation = lame_fields(material_ids, lame_table)
    coeff = jnp.stack([shear, dilatation], 1)[:, :, None].astype(jnp.bfloat16)
    padded, coeff_padded = (
        padded_2(coarse_basis, (("narrow", 3),), 1),
        padded_2(coeff, (("narrow", 3),), 1),
    )
    padded = padded.astype(jnp.float32)
    image = operator_image(padded, coeff_padded.astype(jnp.float32))
    partial_sum = galerkin_of(padded[:, :, :, 1:-1], image)
    galerkin = lax.psum(partial_sum, "narrow")
    slots = (coarse_ids[:, :, None] == jnp.arange(block)[None, None, :]).astype(jnp.float32)
    spread = jnp.einsum("sab,sbc->sac", galerkin, slots, precision=lax.Precision.HIGHEST)
    added = jnp.einsum("sar,sac->rc", slots, spread, precision=lax.Precision.HIGHEST)
    assemble_here = (wide_index == narrow_index * stride) & (narrow_index >= owner)
    base = coarse_slab.astype(jnp.float32)
    base = base.at[:block].add(jnp.where(assemble_here, added, 0.0))
    diagonal = broadcast(base[:block], "wide", owner * stride)
    lower, inverse = diagonal_factor(diagonal)

    def owned():
        return panel_factor(coarse_slab, lower, inverse, wide_index, owner, stride)

    def empty_panel():
        return jnp.zeros(coarse_slab.shape, jnp.bfloat16)

    local_factor = lax.cond(narrow_index == owner, owned, empty_panel)
    factor = broadcast(local_factor, "narrow", owner)
    rows_needed = broadcast(factor[:block], "wide", narrow_index * stride)

    def updated():
        return base - jnp.einsum(
            "rk,ck->rc", factor, rows_needed, preferred_element_type=jnp.float32
        )

    def unchanged():
        return base

    result = lax.cond(narrow_index > owner, updated, unchanged)
    result = jnp.where(narrow_index == owner, factor.astype(jnp.float32), result)
    return (result.astype(jnp.bfloat16), galerkin)


def solution(mesh):
    return jax.shard_map(
        on_device,
        mesh=mesh,
        in_specs=(
            P("wide", None, None, "narrow", None, None),
            P("wide", "narrow", None, None),
            P(),
            P("wide", None),
            P("wide", "narrow"),
            P(),
        ),
        out_specs=(P("wide", "narrow"), P("wide", None, None)),
        check_vma=False,
    )
```

profile of v0, /device:TPU:32, one launch (start us, length us, event | category | flops | bytes accessed | tf_op | source)
XLA Modules:
  0.0 716.5 jit_solution(17513806060626854294)
XLA Ops:
  7.2 2.1 fusion.63
  9.3 1.8 fusion.64
  11.1 10.8 %select_convert_fusion.2 = (bf16[2,4,8,128]{3,2,1,0:T(8,128)(2,1)S(1)}, pred[2,4,8,128]{3,2,1,0:T(8,128)(4,1)S(1)}, pred[2,4,8,128]{3,2,1,0:T(8,128)(4,1)S(1)}, ...) fusion(bf16[]{:T(256)} %bitcast.16, ...), kind=kLoop, calls=%fused_computation.93 | loop fusion | flops 262144 | bytes 180256 | tf_op jit(solution)/shard_map/convert.7
  21.9 10.2 %select_convert_fusion.1 = bf16[2,4,8,128]{3,2,1,0:T(8,128)(2,1)S(1)} fusion(pred[2,4,8,128]{3,2,1,0:T(8,128)(4,1)S(1)} %get-tuple-element.65, pred[2,4,8,128]{3,2,1,0:T(8,128)(4,1)S(1)} %get-tuple-element.64, pred[2,4,8,128]{3,2,1,0:T(8,128)(4,1)S(1)} %get-tuple-element.63, pred[2,4,8,128]{3,2,1,0:T(8,128)(4,1)S(1)} %get-tuple-element.62, ...), kind=kLoop, calls=%fused_computation.92 | loop fusion | flops 131072 | bytes 147488 | tf_op jit(solution)/shard_map/convert.6
  32.7 4.9 collective-permute-start
  37.7 3.3 collective-permute-start.1
  41.0 2.1 fusion.60
  43.1 4.0 collective-permute-start.2
  47.1 4.2 collective-permute-start.3
  53.6 7.6 %reshape.222 = bf16[2,96,12288]{2,1,0:T(8,128)(2,1)} reshape(bf16[2,96,3,4,8,128]{5,4,3,2,1,0:T(8,128)(2,1)} %param.12) | data formatting | bytes 9437184 | tf_op jit(solution)/shard_map/reshape | solution.py:78
  63.7 33.3 %collective-permute-done.2 = bf16[2,96,3,1,8,128]{5,4,3,2,1,0:T(8,128)(2,1)S(1)} collective-permute-done((bf16[2,96,3,1,8,128]{5,4,3,2,1,0:T(8,128)(2,1)S(1)}, bf16[2,96,3,1,8,128]{5,4,3,2,1,0:T(8,128)(2,1)S(1)}, u32[]{:S(2)}, u32[]{:S(2)}) %collective-permute-start.2) | collective-permute-done | bytes 1179680 | tf_op jit(solution)/shard_map/ppermute | solution.py:14
  97.0 2.9 collective-permute-done.3
  99.9 9.3 %maximum_convert_fusion = f32[2,96,3,6,8,128]{5,4,3,2,1,0:T(8,128)} fusion(bf16[2,96,3,1,8,128]{5,4,3,2,1,0:T(8,128)(2,1)} %collective-permute-done.3, bf16[2,96,3,4,8,128]{5,4,3,2,1,0:T(8,128)(2,1)} %param.12, bf16[2,96,3,1,8,128]{5,4,3,2,1,0:T(8,128)(2,1)S(1)} %collective-permute-done.2), kind=kLoop, calls=%fused_computation.16 | loop fusion | flops 10616832 | bytes 21233664 | tf_op jit(solution)/shard_map/convert_element_type | solution.py:115
  109.2 14.4 %fusion.58 = (f32[2,96,3,4,7,128]{5,4,3,2,1,0:T(8,128)}, f32[2,96,3,4,7,128]{5,4,3,2,1,0:T(8,128)}) fusion(f32[2,96,3,6,8,128]{5,4,3,2,1,0:T(8,128)} %maximum_convert_fusion), kind=kLoop, calls=%fused_computation.123 | loop fusion | bytes 33030144 | tf_op jit(solution)/shard_map/slice | solution.py:45
  123.6 2.5 copy-done
  126.1 8.2 %fusion.59 = (f32[2,96,3,4,8,127]{5,4,3,2,1,0:T(8,128)}, f32[2,96,3,4,8,127]{5,4,3,2,1,0:T(8,128)}) fusion(f32[2,96,3,6,8,128]{5,4,3,2,1,0:T(8,128)S(1)} %copy-done), kind=kLoop, calls=%fused_computation.124 | loop fusion | bytes 37453824 | tf_op jit(solution)/shard_map/slice | solution.py:45
  134.3 27.3 %fusion.9 = f32[2,96,3,4,8,128]{5,4,3,2,1,0:T(8,128)} fusion(f32[2,96,3,6,8,128]{5,4,3,2,1,0:T(8,128)} %maximum_convert_fusion, f32[2,96,3,4,8,127]{5,4,3,2,1,0:T(8,128)} %get-tuple-element.71, f32[2,96,3,4,8,127]{5,4,3,2,1,0:T(8,128)} %get-tuple-element.70, f32[2,96,3,4,7,128]{5,4,3,2,1,0:T(8,128)} %get-tuple-element.69, ...), kind=kLoop, calls=%fused_computation.13 | loop fusion | flops 40108032 | bytes 73580544 | tf_op jit(solution)/shard_map/add | solution.py:70
  161.6 10.1 %reshape.221 = f32[2,96,12288]{2,1,0:T(8,128)} reshape(f32[2,96,3,4,8,128]{5,4,3,2,1,0:T(8,128)} %fusion.9) | data formatting | bytes 18874368 | tf_op jit(solution)/shard_map/reshape | solution.py:79
  171.7 10.1 %convolution_bitcast_fusion = f32[2,96,96]{1,2,0:T(8,128)} fusion(f32[2,96,12288]{2,1,0:T(8,128)} %reshape.221, bf16[2,96,12288]{2,1,0:T(8,128)(2,1)} %reshape.222), kind=kOutput, calls=%fused_computation.19 | convolution fusion | flops 2717908992 | bytes 14229504 | tf_op jit(solution)/shard_map/sak,sbk->sab/dot_general | solution.py:76
  182.5 1.6 convert_element_type.93
  184.1 159.0 %all-reduce.13.cloned.1.call-done = f32[2,96,96]{1,2,0:T(8,128)} async-done(((f32[2,96,96]{1,2,0:T(8,128)}), f32[2,96,96]{1,2,0:T(8,128)}) %all-reduce.13.cloned.1.call-update) | async-done | bytes 73744 | tf_op jit(solution)/shard_map/psum | solution.py:118
  343.1 1.2 fusion.13
  345.4 109.8 %all-reduce.15.cloned.1.call-done = f32[128,128]{1,0:T(8,128)} async-done(((f32[128,128]{1,0:T(8,128)}), f32[128,128]{1,0:T(8,128)}) %all-reduce.15.cloned.1.call-update) | async-done | bytes 65552 | tf_op jit(solution)/shard_map/psum | solution.py:22
  455.2 0.9 copy.8
  457.1 11.7 %cholesky.16 = f32[128,128]{1,0:T(8,128)S(1)} custom-call(f32[128,128]{1,0:T(8,128)S(1)} %fusion.16), custom_call_target="Cholesky" | custom-call | tf_op jit(solution)/shard_map/jit(cholesky)/cholesky | solution.py:86
  470.2 9.8 %custom-call.6 = f32[1,128,128]{1,2,0:T(8,128)S(1)} custom-call(f32[1,128,128]{2,1,0:T(8,128)S(1)} %get-tuple-element.47), custom_call_target="InvertDiagBlocksLowerTriangular" | custom-call | tf_op jit(solution)/shard_map/triangular_solve | solution.py:27
  480.2 1.4 conditional.2
  480.3 1.3 broadcast.208
  481.6 1.2 broadcast_select_fusion
  483.6 169.8 %all-reduce.17.cloned.1.call-done = bf16[6144,128]{1,0:T(8,128)(2,1)} async-done(((bf16[6144,128]{1,0:T(8,128)(2,1)}), bf16[6144,128]{1,0:T(8,128)(2,1)}) %all-reduce.17.cloned.1.call-update) | async-done | bytes 1572880 | tf_op jit(solution)/shard_map/psum | solution.py:22
  654.2 52.9 %psum.31 = bf16[128,128]{1,0:T(8,128)(2,1)S(1)} all-reduce(bf16[128,128]{1,0:T(8,128)(2,1)S(1)} %slice_select_fusion), channel_id=1, replica_groups=mesh['wide'=16,'narrow'=16] {'wide'}, use_global_device_ids=true, to_apply=%region_7.8 | all-reduce | flops 16384 | bytes 65536 | tf_op jit(solution)/shard_map/psum | solution.py:22
  707.1 2.9 select_convert_fusion
  (37 shorter events, 10.6 us)
Async XLA Ops:
  7.2 336.0 %all-reduce.13.cloned.1.call-start = ((), (), s32[]{:S(2)}) async-start(), calls=%async_computation | async-start | bytes 196608 | tf_op jit(solution)/shard_map/psum | solution.py:118
  32.7 28.5 %collective-permute-start = (bf16[2,2,1,1,8,128]{5,4,3,0,1,2:T(8,128)(2,1)}, bf16[2,2,1,1,8,128]{5,4,3,0,1,2:T(8,128)(2,1)S(1)}, u32[]{:S(2)}, u32[]{:S(2)}) collective-permute-start(bf16[2,2,1,1,8,128]{5,4,3,0,1,2:T(8,128)(2,1)} %get-tuple-element.96), channel_id=1, source_target_pairs={{0,1},{1,2},{2,3},{3,4},{4,5},{5,6},{6,7},{7,8},{8,9},{9,10},{10,1... | collective-permute-start | bytes 24584 | tf_op jit(solution)/shard_map/ppermute | solution.py:14
  37.7 23.5 %collective-permute-start.1 = (bf16[2,2,1,1,8,128]{5,4,3,0,1,2:T(8,128)(2,1)}, bf16[2,2,1,1,8,128]{5,4,3,0,1,2:T(8,128)(2,1)S(1)}, u32[]{:S(2)}, u32[]{:S(2)}) collective-permute-start(bf16[2,2,1,1,8,128]{5,4,3,0,1,2:T(8,128)(2,1)} %get-tuple-element.97), channel_id=1, source_target_pairs={{1,0},{2,1},{3,2},{4,3},{5,4},{6,5},{7,6},{8,7},{9,8},{10,9},{11,1... | collective-permute-start | bytes 24584 | tf_op jit(solution)/shard_map/ppermute | solution.py:15
  43.1 54.0 %collective-permute-start.2 = (bf16[2,96,3,1,8,128]{5,4,3,2,1,0:T(8,128)(2,1)S(1)}, bf16[2,96,3,1,8,128]{5,4,3,2,1,0:T(8,128)(2,1)S(1)}, u32[]{:S(2)}, u32[]{:S(2)}) collective-permute-start(bf16[2,96,3,1,8,128]{5,4,3,2,1,0:T(8,128)(2,1)S(1)} %get-tuple-element.72), channel_id=1, source_target_pairs={{0,1},{1,2},{2,3},{3,4},{4,5},{5,6},{6,7},{7,8},{8,9},{9,10},{10,1... | collective-permute-start | bytes 3538952 | tf_op jit(solution)/shard_map/ppermute | solution.py:14
  47.1 52.8 %collective-permute-start.3 = (bf16[2,96,3,1,8,128]{5,4,3,2,1,0:T(8,128)(2,1)S(1)}, bf16[2,96,3,1,8,128]{5,4,3,2,1,0:T(8,128)(2,1)}, u32[]{:S(2)}, u32[]{:S(2)}) collective-permute-start(bf16[2,96,3,1,8,128]{5,4,3,2,1,0:T(8,128)(2,1)S(1)} %get-tuple-element.73), channel_id=1, source_target_pairs={{1,0},{2,1},{3,2},{4,3},{5,4},{6,5},{7,6},{8,7},{9,8},{10,9},{11,1... | collective-permute-start | bytes 3538952 | tf_op jit(solution)/shard_map/ppermute | solution.py:15
  109.2 16.9 %copy-start = (f32[2,96,3,6,8,128]{5,4,3,2,1,0:T(8,128)S(1)}, f32[2,96,3,6,8,128]{5,4,3,2,1,0:T(8,128)}, u32[]{:S(2)}) copy-start(f32[2,96,3,6,8,128]{5,4,3,2,1,0:T(8,128)} %maximum_convert_fusion) | copy-start | bytes 42467332
  171.7 171.4 %copy-start.2 = (s32[2,96]{1,0:T(2,128)S(1)}, s32[2,96]{1,0:T(2,128)}, u32[]{:S(2)}) copy-start(s32[2,96]{1,0:T(2,128)} %param.15) | copy-start | bytes 2308
  181.8 273.4 %all-reduce.15.cloned.1.call-start = ((), (), s32[]{:S(2)}) async-start(), calls=%async_computation.1 | async-start | bytes 131072 | tf_op jit(solution)/shard_map/psum | solution.py:22
  345.4 308.0 %all-reduce.17.cloned.1.call-start = ((), (), s32[]{:S(2)}) async-start(), calls=%async_computation.2 | async-start | bytes 3145728 | tf_op jit(solution)/shard_map/psum | solution.py:22
  480.2 2.7 copy-start.1
Sparse Core Ops, SparseCore 0:
  181.9 161.1 all-reduce.12
  346.3 108.8 all-reduce.14
  483.0 170.3 all-reduce.16
where the time goes:
time: 718 us; the launch traced here: 716 us
  waiting for transfers between devices  475 us (66%)
  other arithmetic  93.7 us (13%)
  blocking collectives  52.9 us (7%)
  local copies, waits for them, and re-layouts  52 us (7%)
  starting transfers between devices  16.6 us (2%)
  between operations  14.6 us (2%)
  matrix products  11.9 us (2%)
    psum x2, waiting for transfers between devices, broadcast(): return lax.psum(kept, axis)  280 us
    psum x1, waiting for transfers between devices, on_device(): galerkin = lax.psum(partial_sum, 'narrow')  159 us
    psum x1, blocking collectives, broadcast(): return lax.psum(kept, axis)  52.9 us
    ppermute x2, waiting for transfers between devices, padded_2(): before = lax.ppermute(last, axis, up)  33.3 us
    add x1, other arithmetic, operator_image(): image + face_weight(coeff_centre, other_coeff, direction) * (centre - other)  27.3 us
    slice x4, local copies, waits for them, and re-layouts, shifted(): lax.slice_in_dim(field, 1, length, axis=axis)  22.7 us
    another operation x2, other arithmetic  21 us
  transfers between devices with their start and end apart: 7, of which 5 were waited for; matrix products, arithmetic and copies ran while one was open for 2% of the time, Pallas kernels for 0%

commit v1 on v0

--- a/solution.py
+++ b/solution.py
@@ -115,7 +115,8 @@
     padded = padded.astype(jnp.float32)
     image = operator_image(padded, coeff_padded.astype(jnp.float32))
     partial_sum = galerkin_of(padded[:, :, :, 1:-1], image)
-    galerkin = lax.psum(partial_sum, "narrow")
+    parts = lax.all_gather(partial_sum, "narrow", axis=0, tiled=False)
+    galerkin = parts.sum(axis=0)
     slots = (coarse_ids[:, :, None] == jnp.arange(block)[None, None, :]).astype(jnp.float32)
     spread = jnp.einsum("sab,sbc->sac", galerkin, slots, precision=lax.Precision.HIGHEST)
     added = jnp.einsum("sar,sac->rc", slots, spread, precision=lax.Precision.HIGHEST)

time: 718 us -> 642 us (0.89)
  waiting for transfers between devices: 475 us -> 399 us
    psum x1 -> x0, waiting for transfers between devices: 159 us -> none  [on_device(): galerkin = lax.psum(partial_sum, 'narrow')]
    all_gather x0 -> x1, waiting for transfers between devices: none -> 82.4 us  [on_device(): parts = lax.all_gather(partial_sum, 'narrow', axis=0, tiled=False)]
  transfers between devices with their start and end apart: 7 -> 7, of which waited for: 5 -> 5; matrix products, arithmetic and copies ran while one was open for 2% -> 3% of each run, Pallas kernels for 0% -> 0%
where the time goes in v1:
time: 642 us; the launch traced here: 641 us
  waiting for transfers between devices  399 us (62%)
  other arithmetic  95.2 us (15%)
  blocking collectives  52.9 us (8%)
  local copies, waits for them, and re-layouts  52 us (8%)
  starting transfers between devices  16.6 us (3%)
  between operations  14.6 us (2%)
  matrix products  10.3 us (2%)
    psum x2, waiting for transfers between devices, broadcast(): return lax.psum(kept, axis)  280 us
    all_gather x1, waiting for transfers between devices, on_device(): parts = lax.all_gather(partial_sum, 'narrow', axis=0, tiled=False)  82.4 us
    psum x1, blocking collectives, broadcast(): return lax.psum(kept, axis)  52.9 us
    ppermute x2, waiting for transfers between devices, padded_2(): before = lax.ppermute(last, axis, up)  33.3 us
    add x1, other arithmetic, operator_image(): image + face_weight(coeff_centre, other_coeff, direction) * (centre - other)  27.3 us
    slice x4, local copies, waits for them, and re-layouts, shifted(): lax.slice_in_dim(field, 1, length, axis=axis)  22.7 us
    another operation x2, other arithmetic  21 us
  transfers between devices with their start and end apart: 7, of which 5 were waited for; matrix products, arithmetic and copies ran while one was open for 3% of the time, Pallas kernels for 0%

profile of v1, /device:TPU:32, one launch (start us, length us, event | category | flops | bytes accessed | tf_op | source)
XLA Modules:
  0.0 640.8 jit_solution(8836670541641481512)
XLA Ops:
  7.2 2.1 fusion.63
  9.3 1.8 fusion.64
  11.1 10.8 %select_convert_fusion.2 = (bf16[2,4,8,128]{3,2,1,0:T(8,128)(2,1)S(1)}, pred[2,4,8,128]{3,2,1,0:T(8,128)(4,1)S(1)}, pred[2,4,8,128]{3,2,1,0:T(8,128)(4,1)S(1)}, ...) fusion(bf16[]{:T(256)} %bitcast.16, ...), kind=kLoop, calls=%fused_computation.93 | loop fusion | flops 262144 | bytes 180256 | tf_op jit(solution)/shard_map/convert.7
  21.9 10.2 %select_convert_fusion.1 = bf16[2,4,8,128]{3,2,1,0:T(8,128)(2,1)S(1)} fusion(pred[2,4,8,128]{3,2,1,0:T(8,128)(4,1)S(1)} %get-tuple-element.65, pred[2,4,8,128]{3,2,1,0:T(8,128)(4,1)S(1)} %get-tuple-element.64, pred[2,4,8,128]{3,2,1,0:T(8,128)(4,1)S(1)} %get-tuple-element.63, pred[2,4,8,128]{3,2,1,0:T(8,128)(4,1)S(1)} %get-tuple-element.62, ...), kind=kLoop, calls=%fused_computation.92 | loop fusion | flops 131072 | bytes 147488 | tf_op jit(solution)/shard_map/convert.6
  32.7 4.9 collective-permute-start
  37.7 3.3 collective-permute-start.1
  41.0 2.1 fusion.60
  43.1 4.0 collective-permute-start.2
  47.1 4.2 collective-permute-start.3
  53.6 7.6 %reshape.222 = bf16[2,96,12288]{2,1,0:T(8,128)(2,1)} reshape(bf16[2,96,3,4,8,128]{5,4,3,2,1,0:T(8,128)(2,1)} %param.12) | data formatting | bytes 9437184 | tf_op jit(solution)/shard_map/reshape | solution.py:78
  63.7 33.3 %collective-permute-done.2 = bf16[2,96,3,1,8,128]{5,4,3,2,1,0:T(8,128)(2,1)S(1)} collective-permute-done((bf16[2,96,3,1,8,128]{5,4,3,2,1,0:T(8,128)(2,1)S(1)}, bf16[2,96,3,1,8,128]{5,4,3,2,1,0:T(8,128)(2,1)S(1)}, u32[]{:S(2)}, u32[]{:S(2)}) %collective-permute-start.2) | collective-permute-done | bytes 1179680 | tf_op jit(solution)/shard_map/ppermute | solution.py:14
  97.0 2.9 collective-permute-done.3
  99.9 9.3 %maximum_convert_fusion = f32[2,96,3,6,8,128]{5,4,3,2,1,0:T(8,128)} fusion(bf16[2,96,3,1,8,128]{5,4,3,2,1,0:T(8,128)(2,1)} %collective-permute-done.3, bf16[2,96,3,4,8,128]{5,4,3,2,1,0:T(8,128)(2,1)} %param.12, bf16[2,96,3,1,8,128]{5,4,3,2,1,0:T(8,128)(2,1)S(1)} %collective-permute-done.2), kind=kLoop, calls=%fused_computation.16 | loop fusion | flops 10616832 | bytes 21233664 | tf_op jit(solution)/shard_map/convert_element_type | solution.py:115
  109.2 14.4 %fusion.58 = (f32[2,96,3,4,7,128]{5,4,3,2,1,0:T(8,128)}, f32[2,96,3,4,7,128]{5,4,3,2,1,0:T(8,128)}) fusion(f32[2,96,3,6,8,128]{5,4,3,2,1,0:T(8,128)} %maximum_convert_fusion), kind=kLoop, calls=%fused_computation.123 | loop fusion | bytes 33030144 | tf_op jit(solution)/shard_map/slice | solution.py:45
  123.6 2.5 copy-done
  126.1 8.2 %fusion.59 = (f32[2,96,3,4,8,127]{5,4,3,2,1,0:T(8,128)}, f32[2,96,3,4,8,127]{5,4,3,2,1,0:T(8,128)}) fusion(f32[2,96,3,6,8,128]{5,4,3,2,1,0:T(8,128)S(1)} %copy-done), kind=kLoop, calls=%fused_computation.124 | loop fusion | bytes 37453824 | tf_op jit(solution)/shard_map/slice | solution.py:45
  134.3 27.3 %fusion.9 = f32[2,96,3,4,8,128]{5,4,3,2,1,0:T(8,128)} fusion(f32[2,96,3,6,8,128]{5,4,3,2,1,0:T(8,128)} %maximum_convert_fusion, f32[2,96,3,4,8,127]{5,4,3,2,1,0:T(8,128)} %get-tuple-element.71, f32[2,96,3,4,8,127]{5,4,3,2,1,0:T(8,128)} %get-tuple-element.70, f32[2,96,3,4,7,128]{5,4,3,2,1,0:T(8,128)} %get-tuple-element.69, ...), kind=kLoop, calls=%fused_computation.13 | loop fusion | flops 40108032 | bytes 73580544 | tf_op jit(solution)/shard_map/add | solution.py:70
  161.6 10.1 %reshape.221 = f32[2,96,12288]{2,1,0:T(8,128)} reshape(f32[2,96,3,4,8,128]{5,4,3,2,1,0:T(8,128)} %fusion.9) | data formatting | bytes 18874368 | tf_op jit(solution)/shard_map/reshape | solution.py:79
  171.7 9.4 %convolution_bitcast_fusion = f32[2,96,96]{1,2,0:T(8,128)S(1)} fusion(f32[2,96,12288]{2,1,0:T(8,128)} %reshape.221, bf16[2,96,12288]{2,1,0:T(8,128)(2,1)} %reshape.222), kind=kOutput, calls=%fused_computation.19 | convolution fusion | flops 2717908992 | bytes 14229504 | tf_op jit(solution)/shard_map/sak,sbk->sab/dot_general | solution.py:76
  182.6 1.6 convert_element_type.93
  184.2 82.4 %all-gather.3.cloned.1.call-done = f32[32,96,96]{2,1,0:T(8,128)} async-done(((f32[2,96,96]{2,1,0:T(8,128)}), f32[32,96,96]{2,1,0:T(8,128)}) %all-gather.3.cloned.1.call-update) | async-done | bytes 1179664 | tf_op jit(solution)/shard_map/all_gather | solution.py:118
  266.7 1.5 reduce_sum.9
  269.6 110.0 %all-reduce.12.cloned.1.call-done = f32[128,128]{1,0:T(8,128)} async-done(((f32[128,128]{1,0:T(8,128)}), f32[128,128]{1,0:T(8,128)}) %all-reduce.12.cloned.1.call-update) | async-done | bytes 65552 | tf_op jit(solution)/shard_map/psum | solution.py:22
  379.6 0.9 copy.12
  381.5 11.7 %cholesky.16 = f32[128,128]{1,0:T(8,128)S(1)} custom-call(f32[128,128]{1,0:T(8,128)S(1)} %fusion.16), custom_call_target="Cholesky" | custom-call | tf_op jit(solution)/shard_map/jit(cholesky)/cholesky | solution.py:86
  394.6 9.8 %custom-call.6 = f32[1,128,128]{1,2,0:T(8,128)S(1)} custom-call(f32[1,128,128]{2,1,0:T(8,128)S(1)} %get-tuple-element.47), custom_call_target="InvertDiagBlocksLowerTriangular" | custom-call | tf_op jit(solution)/shard_map/triangular_solve | solution.py:27
  404.7 1.4 conditional.2
  404.7 1.3 broadcast.208
  406.0 1.2 broadcast_select_fusion
  407.3 170.4 %all-reduce.14.cloned.1.call-done = bf16[6144,128]{1,0:T(8,128)(2,1)} async-done(((bf16[6144,128]{1,0:T(8,128)(2,1)}), bf16[6144,128]{1,0:T(8,128)(2,1)}) %all-reduce.14.cloned.1.call-update) | async-done | bytes 1572880 | tf_op jit(solution)/shard_map/psum | solution.py:22
  578.5 52.9 %psum.23 = bf16[128,128]{1,0:T(8,128)(2,1)S(1)} all-reduce(bf16[128,128]{1,0:T(8,128)(2,1)S(1)} %slice_select_fusion), channel_id=1, replica_groups=mesh['wide'=16,'narrow'=16] {'wide'}, use_global_device_ids=true, to_apply=%region_7.8 | all-reduce | flops 16384 | bytes 65536 | tf_op jit(solution)/shard_map/psum | solution.py:22
  631.4 2.9 select_convert_fusion
  (38 shorter events, 10.8 us)
Async XLA Ops:
  7.2 259.5 %all-gather.3.cloned.1.call-start = ((), (), s32[]{:S(2)}) async-start(), calls=%async_computation.2 | async-start | bytes 1671168 | tf_op jit(solution)/shard_map/all_gather | solution.py:118
  32.7 28.5 %collective-permute-start = (bf16[2,2,1,1,8,128]{5,4,3,0,1,2:T(8,128)(2,1)}, bf16[2,2,1,1,8,128]{5,4,3,0,1,2:T(8,128)(2,1)S(1)}, u32[]{:S(2)}, u32[]{:S(2)}) collective-permute-start(bf16[2,2,1,1,8,128]{5,4,3,0,1,2:T(8,128)(2,1)} %get-tuple-element.96), channel_id=1, source_target_pairs={{0,1},{1,2},{2,3},{3,4},{4,5},{5,6},{6,7},{7,8},{8,9},{9,10},{10,1... | collective-permute-start | bytes 24584 | tf_op jit(solution)/shard_map/ppermute | solution.py:14
  37.7 23.5 %collective-permute-start.1 = (bf16[2,2,1,1,8,128]{5,4,3,0,1,2:T(8,128)(2,1)}, bf16[2,2,1,1,8,128]{5,4,3,0,1,2:T(8,128)(2,1)S(1)}, u32[]{:S(2)}, u32[]{:S(2)}) collective-permute-start(bf16[2,2,1,1,8,128]{5,4,3,0,1,2:T(8,128)(2,1)} %get-tuple-element.97), channel_id=1, source_target_pairs={{1,0},{2,1},{3,2},{4,3},{5,4},{6,5},{7,6},{8,7},{9,8},{10,9},{11,1... | collective-permute-start | bytes 24584 | tf_op jit(solution)/shard_map/ppermute | solution.py:15
  43.1 54.0 %collective-permute-start.2 = (bf16[2,96,3,1,8,128]{5,4,3,2,1,0:T(8,128)(2,1)S(1)}, bf16[2,96,3,1,8,128]{5,4,3,2,1,0:T(8,128)(2,1)S(1)}, u32[]{:S(2)}, u32[]{:S(2)}) collective-permute-start(bf16[2,96,3,1,8,128]{5,4,3,2,1,0:T(8,128)(2,1)S(1)} %get-tuple-element.72), channel_id=1, source_target_pairs={{0,1},{1,2},{2,3},{3,4},{4,5},{5,6},{6,7},{7,8},{8,9},{9,10},{10,1... | collective-permute-start | bytes 3538952 | tf_op jit(solution)/shard_map/ppermute | solution.py:14
  47.1 52.8 %collective-permute-start.3 = (bf16[2,96,3,1,8,128]{5,4,3,2,1,0:T(8,128)(2,1)S(1)}, bf16[2,96,3,1,8,128]{5,4,3,2,1,0:T(8,128)(2,1)}, u32[]{:S(2)}, u32[]{:S(2)}) collective-permute-start(bf16[2,96,3,1,8,128]{5,4,3,2,1,0:T(8,128)(2,1)S(1)} %get-tuple-element.73), channel_id=1, source_target_pairs={{1,0},{2,1},{3,2},{4,3},{5,4},{6,5},{7,6},{8,7},{9,8},{10,9},{11,1... | collective-permute-start | bytes 3538952 | tf_op jit(solution)/shard_map/ppermute | solution.py:15
  109.2 16.9 %copy-start = (f32[2,96,3,6,8,128]{5,4,3,2,1,0:T(8,128)S(1)}, f32[2,96,3,6,8,128]{5,4,3,2,1,0:T(8,128)}, u32[]{:S(2)}) copy-start(f32[2,96,3,6,8,128]{5,4,3,2,1,0:T(8,128)} %maximum_convert_fusion) | copy-start | bytes 42467332
  171.7 96.5 %copy-start.2 = (s32[2,96]{1,0:T(2,128)S(1)}, s32[2,96]{1,0:T(2,128)}, u32[]{:S(2)}) copy-start(s32[2,96]{1,0:T(2,128)} %param.15) | copy-start | bytes 2308
  181.9 197.7 %all-reduce.12.cloned.1.call-start = ((), (), s32[]{:S(2)}) async-start(), calls=%async_computation | async-start | bytes 131072 | tf_op jit(solution)/shard_map/psum | solution.py:22
  268.2 139.1 %copy-start.1 = (f32[2,96,96]{2,1,0:T(8,128)}, f32[2,96,96]{2,1,0:T(8,128)S(1)}, u32[]{:S(2)}) copy-start(f32[2,96,96]{2,1,0:T(8,128)S(1)} %reduce_sum.9) | copy-start | bytes 221188
  269.5 308.2 %all-reduce.14.cloned.1.call-start = ((), (), s32[]{:S(2)}) async-start(), calls=%async_computation.1 | async-start | bytes 3145728 | tf_op jit(solution)/shard_map/psum | solution.py:22
Sparse Core Ops, SparseCore 0:
  182.0 84.6 all-gather.2
  269.9 109.7 all-reduce.11
  407.4 170.2 all-reduce.13
